TPU v7x, 32 devices: a whole 2x2x4 slice. The times are simulated.
32 devices in a mesh: grp: 4 (over z), mem: 8 (over y, x, core).
Axes of the slice: x: 2, y: 2, z: 4, core: 2. Of those that a mesh axis runs over, the one named last changes fastest.
Arguments:
- bin_sketch: bfloat16 [256, 1024], P(('grp', 'mem')), may hold values from -6 to 6
- rep_sketch: bfloat16 [8192, 1024], P(('grp', 'mem')), may hold values from -6 to 6
- bin_profile: bfloat16 [256, 32768], P('grp', 'mem'), may hold values from -6 to 6
- member_profile: bfloat16 [12, 256, 32768], P('grp', None, 'mem'), may hold values from -6 to 6
- bin_routes: int32 [256, 2], P('grp'), may hold values from 0 to 11, all different within a row; in each aligned block of 64 rows (0 to 63, 64 to 127, ...) at most 16 rows name the same one
- owner_slot: int32 [12], replicated, may hold values from 0 to 11, each once
- cluster_sizes: int32 [12], replicated, may hold values from 128 to 256, as said below
Outputs:
- coarse_scores: bfloat16 [256, 8192], P(None, ('grp', 'mem'))
- fine_scores: float32 [256, 2, 256], P('grp', None, 'mem')
Inputs may be any that keep to these rules, and one draw needn't show every extreme that they name: `bin_routes`: within the bins of one index of grp (64 consecutive bins), no cluster is named by more than 16 routes, a bound that some block reaches; the two clusters of a bin differ. `owner_slot`: A permutation. `cluster_sizes`: each a multiple of 128.
All inputs are finite; a program needn't handle non-finite values.
Results may differ from a plain program's by a relative error of at most 0.001.
Values may be sent and summed in bfloat16 or wider, within the bound.
No kernel may reach another device: no remote copies, remote signals or barrier semaphores. Data moves between devices by JAX's collectives and lax.ppermute only.
A program may use at most 128 MiB of HBM per device.

v0:
```python
import jax
import jax.numpy as jnp
from jax import lax
from jax.sharding import PartitionSpec as P

FW = 32768
MOST = 16


def local(
    bin_sketch, rep_sketch, bin_profile, member_profile, bin_routes, owner_slot, cluster_sizes
):
    coarse_scale = bin_sketch.shape[1] ** (-0.5)
    group_rows = lax.all_gather(bin_sketch, "mem", axis=0, tiled=True)
    product = lax.dot_general(
        lax.all_gather(group_rows, "grp", axis=0, tiled=True),
        rep_sketch,
        (((1,), (1,)), ((), ())),
        preferred_element_type=jnp.float32,
    )
    coarse_scores = (product * coarse_scale).astype(jnp.bfloat16)
    rows_here, width_here = bin_profile.shape
    slot_count, members, _ = member_profile.shape
    groups = lax.axis_size("grp")
    cluster_total = owner_slot.shape[0]
    capacity = groups * slot_count * MOST
    route_flat = bin_routes.reshape(-1)
    cluster_ids = jnp.arange(cluster_total, dtype=jnp.int32)
    route_hit = (route_flat[:, None] == cluster_ids[None, :]).astype(jnp.int32)
    storage = jnp.sum(route_hit * owner_slot[None, :], axis=1)
    route_size = jnp.sum(route_hit * cluster_sizes[None, :], axis=1)
    route_rank = jnp.sum((jnp.cumsum(route_hit, axis=0) - route_hit) * route_hit, axis=1)
    slot_index = storage * MOST + route_rank
    source = bin_profile[jnp.arange(route_flat.shape[0], dtype=jnp.int32) // 2]
    outgoing = jnp.zeros((capacity, width_here), jnp.bfloat16).at[slot_index].set(source)
    outgoing = outgoing.reshape(groups, slot_count * MOST, width_here)
    incoming = lax.all_to_all(outgoing, "grp", split_axis=0, concat_axis=0, tiled=True)
    incoming = incoming.reshape(groups, slot_count, MOST, width_here)
    partial_value = jnp.einsum(
        "gsmc,sjc->gsmj", incoming, member_profile, preferred_element_type=jnp.float32
    )
    summed = lax.psum_scatter(partial_value, "mem", scatter_dimension=3, tiled=True)
    returned = lax.all_to_all(summed, "grp", split_axis=0, concat_axis=0, tiled=True)
    member_local = returned.shape[3]
    route_scores = returned.reshape(capacity, member_local)[slot_index] * FW ** (-0.5)
    column = lax.axis_index("mem") * member_local + jnp.arange(member_local, dtype=jnp.int32)
    member_live = column[None, :] < route_size[:, None]
    fine_scores = jnp.where(member_live, route_scores, 0.0).reshape(rows_here, 2, member_local)
    return (coarse_scores, fine_scores)


def solution(mesh):
    return jax.shard_map(
        local,
        mesh=mesh,
        in_specs=(
            P(("grp", "mem"), None),
            P(("grp", "mem"), None),
            P("grp", "mem"),
            P("grp", None, "mem"),
            P("grp", None),
            P(),
            P(),
        ),
        out_specs=(P(None, ("grp", "mem")), P("grp", None, "mem")),
        check_vma=False,
    )
```

profile of v0, /device:TPU:0, one launch (start us, length us, event | category | flops | bytes accessed | tf_op | source)
XLA Modules:
  0.0 133.0 jit_solution(8496143700417119367)
XLA Ops:
  7.2 0.0 copy-start
  7.2 0.8 copy.17
  8.0 0.1 eq.15
  8.2 0.1 fusion.12
  8.3 0.2 reduce_window_sum.11
  8.4 0.9 select_reduce_fusion.2
  9.3 0.0 copy-done
  9.3 6.4 %scatter_custom_fusion = bf16[192,4096]{1,0:T(8,128)(2,1)} fusion(s32[128]{0:T(128)S(1)} %fusion.14, bf16[64,4096]{1,0:T(8,128)(2,1)S(1)} %copy-done, s32[1024]{0:T(1024)S(1)} %pad_clamp_fusion.1, bf16[]{:T(256)} %constant.36.clone.1), kind=kCustom, calls=%fused_computation.9 | custom fusion | bytes 1572866 | tf_op jit(solution)/shard_map/scatter | solution.py:35
  15.7 0.0 copy-start.2
  15.7 6.5 %all-to-all-start = ((bf16[4,48,4096]{2,1,0:T(8,128)(2,1)}), bf16[4,48,4096]{2,1,0:T(8,128)(2,1)S(1)}, u32[]{:S(2)}, u32[]{:S(2)}) async-start(bf16[4,48,4096]{2,1,0:T(8,128)(2,1)} %bitcast.3), calls=%async_computation | async-start | bytes 3145728 | tf_op jit(solution)/shard_map/all_to_all | solution.py:37
  22.2 0.0 reduce-scatter.4.cloned.1.call-start
  22.2 0.0 copy-done.2
  22.2 9.2 %all_gather.6 = bf16[64,1024]{1,0:T(8,128)(2,1)S(1)} all-gather(bf16[8,1024]{1,0:T(8,128)(2,1)S(1)} %copy-done.2), channel_id=1, replica_groups=mesh['grp'=4,'mem'=8] {'mem'}, dimensions={0}, use_global_device_ids=true | all-gather | bytes 147456 | tf_op jit(solution)/shard_map/all_gather | solution.py:14
  31.4 38.1 %all_gather.7 = bf16[256,1024]{1,0:T(8,128)(2,1)S(1)} all-gather(bf16[64,1024]{1,0:T(8,128)(2,1)S(1)} %all_gather.6), channel_id=1, replica_groups=mesh['grp'=4,'mem'=8] {'grp'}, dimensions={0}, use_global_device_ids=true | all-gather | bytes 655360 | tf_op jit(solution)/shard_map/all_gather | solution.py:16
  69.5 0.0 all-to-all-done
  69.5 4.8 %fusion.4 = f32[4,3,16,256]{3,2,0,1:T(8,128)S(1)} fusion(bf16[3,256,4096]{2,1,0:T(8,128)(2,1)} %param.10, bf16[4,3,16,4096]{3,2,1,0:T(8,128)(2,1)S(1)} %bitcast.25), kind=kOutput, calls=%fused_computation.8 | convolution fusion | flops 402653184 | bytes 8060928 | tf_op jit(solution)/shard_map/gsmc,sjc->gsmj/dot_general | solution.py:39
  74.4 0.0 copy-start.1
  74.4 0.7 copy.23
  75.1 1.5 %reshape.132 = f32[256,192]{1,0:T(8,128)} reshape(f32[256,3,4,16]{3,2,1,0:T(4,128)S(1)} %bitcast.24) | data formatting | bytes 393216
  76.6 0.0 reduce-scatter.4.cloned.1.call-update
  76.6 0.0 copy-done.1
  76.6 1.0 fusion.3
  77.6 33.7 %reduce-scatter.4.cloned.1.call-done = f32[32,192]{1,0:T(8,128)} async-done(((f32[256,192]{1,0:T(8,128)}), f32[32,192]{1,0:T(8,128)}) %reduce-scatter.4.cloned.1.call-update) | async-done | bytes 24592
  111.4 0.9 reshape.133
  112.3 0.1 copy.20
  112.4 0.7 reshape.140
  113.1 4.6 %all-to-all-start.1 = ((f32[4,1,1536]{2,1,0:T(1,128)}), f32[4,1,1536]{2,1,0:T(1,128)S(1)}, u32[]{:S(2)}, u32[]{:S(2)}) async-start(f32[4,1,1536]{2,1,0:T(1,128)} %reshape.140), calls=%async_computation.1 | async-start | bytes 49152 | tf_op jit(solution)/shard_map/all_to_all | solution.py:43
  117.7 0.1 lt.38
  117.9 0.1 copy.18
  117.9 5.4 %all-to-all-done.1 = f32[4,1,1536]{2,1,0:T(1,128)S(1)} async-done(((f32[4,1,1536]{2,1,0:T(1,128)}), f32[4,1,1536]{2,1,0:T(1,128)S(1)}, u32[]{:S(2)}, u32[]{:S(2)}) %all-to-all-start.1) | async-done | bytes 24608 | tf_op jit(solution)/shard_map/all_to_all | solution.py:43
  123.4 0.5 broadcast.125
  123.9 0.7 reduce
  124.6 0.1 reshape.141
  124.7 0.6 gather_fusion
  125.3 0.1 copy.21
  125.4 0.7 compare_select_fusion
  (6 shorter events, 0.0 us)
Async XLA Ops:
  7.2 2.2 %copy-start = (bf16[64,4096]{1,0:T(8,128)(2,1)S(1)}, bf16[64,4096]{1,0:T(8,128)(2,1)}, u32[]{:S(2)}) copy-start(bf16[64,4096]{1,0:T(8,128)(2,1)} %param.9) | copy-start | bytes 1572868
  15.7 6.5 %copy-start.2 = (bf16[8,1024]{1,0:T(8,128)(2,1)S(1)}, bf16[8,1024]{1,0:T(8,128)(2,1)}, u32[]{:S(2)}) copy-start(bf16[8,1024]{1,0:T(8,128)(2,1)} %param.7) | copy-start | bytes 49156
  15.7 53.8 %all-to-all-start = ((bf16[4,48,4096]{2,1,0:T(8,128)(2,1)}), bf16[4,48,4096]{2,1,0:T(8,128)(2,1)S(1)}, u32[]{:S(2)}, u32[]{:S(2)}) async-start(bf16[4,48,4096]{2,1,0:T(8,128)(2,1)} %bitcast.3), calls=%async_computation | async-start | bytes 3145728 | tf_op jit(solution)/shard_map/all_to_all | solution.py:37
  22.2 89.2 %reduce-scatter.4.cloned.1.call-start = ((), (), s32[]{:S(2)}) async-start(), calls=%async_computation.3 | async-start | bytes 294912
  74.4 2.3 %copy-start.1 = (bf16[256,1024]{1,0:T(8,128)(2,1)S(1)}, bf16[256,1024]{1,0:T(8,128)(2,1)}, u32[]{:S(2)}) copy-start(bf16[256,1024]{1,0:T(8,128)(2,1)} %param.8) | copy-start | bytes 1572868
  113.1 10.2 %all-to-all-start.1 = ((f32[4,1,1536]{2,1,0:T(1,128)}), f32[4,1,1536]{2,1,0:T(1,128)S(1)}, u32[]{:S(2)}, u32[]{:S(2)}) async-start(f32[4,1,1536]{2,1,0:T(1,128)} %reshape.140), calls=%async_computation.1 | async-start | bytes 49152 | tf_op jit(solution)/shard_map/all_to_all | solution.py:43
Sparse Core Ops, SparseCore 0:
  76.7 34.6 reduce-scatter.3
where the time goes:
time: 133 us
  blocking collectives  47.3 us (36%)
  waiting for transfers between devices  39.2 us (29%)
  between operations  14.1 us (11%)
  local copies, waits for them, and re-layouts  12.8 us (10%)
  starting transfers between devices  11.1 us (8%)
  matrix products  5.81 us (4%)
  other arithmetic  2.59 us (2%)
    all_gather x1, blocking collectives, local(): lax.all_gather(group_rows, 'grp', axis=0, tiled=True)  38.1 us
    unnamed x2, waiting for transfers between devices  33.8 us
    all_gather x1, blocking collectives, local(): group_rows = lax.all_gather(bin_sketch, 'mem', axis=0, tiled=True)  9.22 us
    all_to_all x1, starting transfers between devices, local(): lax.all_to_all(outgoing, 'grp', split_axis=0, concat_axis=0, tiled=True)  6.48 us
    scatter x1, local copies, waits for them, and re-layouts, local(): jnp.zeros((capacity, width_here), jnp.bfloat16).at[slot_index].set(source)  6.38 us
    all_to_all x1, waiting for transfers between devices, local(): lax.all_to_all(summed, 'grp', split_axis=0, concat_axis=0, tiled=True)  5.43 us
    dot_general x1, matrix products, local(): jnp.einsum('gsmc,sjc->gsmj', incoming, member_profile, preferred_element_...  4.81 us
    unnamed x12, local copies, waits for them, and re-layouts  4.76 us
  transfers between devices with their start and end apart: 3, of which 2 were waited for; matrix products, arithmetic and copies ran while one was open for 1% of the time, Pallas kernels for 0%

commit v1 on v0

--- a/solution.py
+++ b/solution.py
@@ -11,7 +11,16 @@
     bin_sketch, rep_sketch, bin_profile, member_profile, bin_routes, owner_slot, cluster_sizes
 ):
     coarse_scale = bin_sketch.shape[1] ** (-0.5)
-    group_rows = lax.all_gather(bin_sketch, "mem", axis=0, tiled=True)
+    ways = lax.axis_size("mem")
+    up = [(d, (d + 1) % ways) for d in range(ways)]
+    down = [(d, (d - 1) % ways) for d in range(ways)]
+    earlier, later = ([bin_sketch], [bin_sketch])
+    for __2 in range(ways // 2):
+        earlier.append(lax.ppermute(earlier[-1], "mem", up))
+    for __2 in range((ways - 1) // 2):
+        later.append(lax.ppermute(later[-1], "mem", down))
+    line = jnp.concatenate([*earlier[::-1], *later[1:]], axis=0)
+    group_rows = jnp.roll(line, (lax.axis_index("mem") - ways // 2) * bin_sketch.shape[0], axis=0)
     product = lax.dot_general(
         lax.all_gather(group_rows, "grp", axis=0, tiled=True),
         rep_sketch,

time: 133 us -> 121 us (0.910)
  blocking collectives: 47.3 us -> 15.9 us
  waiting for transfers between devices: 39.2 us -> 49.7 us
  starting transfers between devices: 11.1 us -> 19.6 us
    all_gather x1, blocking collectives: 38.1 us -> 15.9 us  [local(): lax.all_gather(group_rows, 'grp', axis=0, tiled=True)]
    all_to_all x1, waiting for transfers between devices: 0.01 us -> 20 us  [local(): lax.all_to_all(outgoing, 'grp', split_axis=0, concat_axis=0, tiled=True)]
    unnamed x2, waiting for transfers between devices: 33.8 us -> 17 us
    all_gather x1 -> x0, blocking collectives: 9.22 us -> none  [local(): group_rows = lax.all_gather(bin_sketch, 'mem', axis=0, tiled=True)]
    ppermute x0 -> x7, starting transfers between devices: none -> 8.53 us  [the longest x3 8.47 us: local(): later.append(lax.ppermute(later[-1], 'mem', down))]
    ppermute x0 -> x7, waiting for transfers between devices: none -> 8.09 us  [the longest x4 7.42 us: local(): earlier.append(lax.ppermute(earlier[-1], 'mem', up))]
    unnamed x12 -> x27, local copies, waits for them, and re-layouts: 4.76 us -> 4.81 us
  transfers between devices with their start and end apart: 3 -> 10, of which waited for: 2 -> 9; matrix products, arithmetic and copies ran while one was open for 1% -> 1% of each run, Pallas kernels for 0% -> 0%
where the time goes in v1:
time: 121 us
  waiting for transfers between devices  49.7 us (41%)
  starting transfers between devices  19.6 us (16%)
  blocking collectives  15.9 us (13%)
  between operations  14.2 us (12%)
  local copies, waits for them, and re-layouts  12.9 us (11%)
  matrix products  5.81 us (5%)
  other arithmetic  2.59 us (2%)
    all_to_all x1, waiting for transfers between devices, local(): lax.all_to_all(outgoing, 'grp', split_axis=0, concat_axis=0, tiled=True)  20 us
    unnamed x2, waiting for transfers between devices  17 us
    all_gather x1, blocking collectives, local(): lax.all_gather(group_rows, 'grp', axis=0, tiled=True)  15.9 us
    ppermute x3, starting transfers between devices, local(): later.append(lax.ppermute(later[-1], 'mem', down))  8.47 us
    ppermute x4, waiting for transfers between devices, local(): earlier.append(lax.ppermute(earlier[-1], 'mem', up))  7.42 us
    all_to_all x1, starting transfers between devices, local(): lax.all_to_all(outgoing, 'grp', split_axis=0, concat_axis=0, tiled=True)  6.48 us
    scatter x1, local copies, waits for them, and re-layouts, local(): jnp.zeros((capacity, width_here), jnp.bfloat16).at[slot_index].set(source)  6.38 us
    dot_general x1, matrix products, local(): jnp.einsum('gsmc,sjc->gsmj', incoming, member_profile, preferred_element_...  4.81 us
  transfers between devices with their start and end apart: 10, of which 9 were waited for; matrix products, arithmetic and copies ran while one was open for 1% of the time, Pallas kernels for 0%

profile of v1, /device:TPU:0, one launch (start us, length us, event | category | flops | bytes accessed | tf_op | source)
XLA Modules:
  0.0 120.8 jit_solution(14597713767743190903)
XLA Ops:
  7.2 0.0 copy-start
  7.2 0.8 copy.17
  8.0 0.1 eq.18
  8.2 0.1 fusion.12
  8.3 0.2 reduce_window_sum.11
  8.4 0.9 select_reduce_fusion.2
  9.3 0.0 copy-done
  9.3 6.4 %scatter_custom_fusion = bf16[192,4096]{1,0:T(8,128)(2,1)} fusion(s32[128]{0:T(128)S(1)} %fusion.14, bf16[64,4096]{1,0:T(8,128)(2,1)S(1)} %copy-done, s32[1024]{0:T(1024)S(1)} %pad_clamp_fusion.1, bf16[]{:T(256)} %constant.62.clone.1), kind=kCustom, calls=%fused_computation.9 | custom fusion | bytes 1572866 | tf_op jit(solution)/shard_map/scatter | solution.py:44
  15.7 0.0 copy-start.2
  15.7 6.5 %all-to-all-start = ((bf16[4,48,4096]{2,1,0:T(8,128)(2,1)}), bf16[4,48,4096]{2,1,0:T(8,128)(2,1)S(1)}, u32[]{:S(2)}, u32[]{:S(2)}) async-start(bf16[4,48,4096]{2,1,0:T(8,128)(2,1)} %bitcast.3), calls=%async_computation | async-start | bytes 3145728 | tf_op jit(solution)/shard_map/all_to_all | solution.py:46
  22.2 0.0 reduce-scatter.4.cloned.1.call-start
  22.2 0.0 copy-done.2
  22.2 0.1 collective-permute-start
  22.3 4.0 %collective-permute-done = bf16[8,1024]{1,0:T(8,128)(2,1)S(1)} collective-permute-done((bf16[8,1024]{1,0:T(8,128)(2,1)S(1)}, bf16[8,1024]{1,0:T(8,128)(2,1)S(1)}, u32[]{:S(2)}, u32[]{:S(2)}) %collective-permute-start) | collective-permute-done | bytes 16416 | tf_op jit(solution)/shard_map/ppermute | solution.py:19
  26.3 0.0 collective-permute-start.1
  26.3 2.6 %collective-permute-start.4 = (bf16[8,1024]{1,0:T(8,128)(2,1)S(1)}, bf16[8,1024]{1,0:T(8,128)(2,1)S(1)}, u32[]{:S(2)}, u32[]{:S(2)}) collective-permute-start(bf16[8,1024]{1,0:T(8,128)(2,1)S(1)} %copy-done.2), channel_id=1, source_target_pairs={{0,7},{1,0},{2,1},{3,2},{4,3},{5,4},{6,5},{7,6},{8,15},{9,8},{10,9... | collective-permute-start | bytes 49160 | tf_op jit(solution)/shard_map/ppermute | solution.py:21
  29.0 1.4 %collective-permute-done.1 = bf16[8,1024]{1,0:T(8,128)(2,1)S(1)} collective-permute-done((bf16[8,1024]{1,0:T(8,128)(2,1)S(1)}, bf16[8,1024]{1,0:T(8,128)(2,1)S(1)}, u32[]{:S(2)}, u32[]{:S(2)}) %collective-permute-start.1) | collective-permute-done | bytes 16416 | tf_op jit(solution)/shard_map/ppermute | solution.py:19
  30.4 0.0 collective-permute-start.2
  30.4 0.0 collective-permute-done.4
  30.4 2.9 %collective-permute-start.5 = (bf16[8,1024]{1,0:T(8,128)(2,1)S(1)}, bf16[8,1024]{1,0:T(8,128)(2,1)S(1)}, u32[]{:S(2)}, u32[]{:S(2)}) collective-permute-start(bf16[8,1024]{1,0:T(8,128)(2,1)S(1)} %collective-permute-done.4), channel_id=1, source_target_pairs={{0,7},{1,0},{2,1},{3,2},{4,3},{5,4},{6,5},{7,6},{8,15},{9,8},{10,9... | collective-permute-start | bytes 49160 | tf_op jit(solution)/shard_map/ppermute | solution.py:21
  33.3 1.1 collective-permute-done.2
  34.5 0.0 collective-permute-start.3
  34.5 0.1 lt.52
  34.6 0.1 copy.18
  34.7 0.1 collective-permute-done.5
  34.8 2.9 %collective-permute-start.6 = (bf16[8,1024]{1,0:T(8,128)(2,1)S(1)}, bf16[8,1024]{1,0:T(8,128)(2,1)S(1)}, u32[]{:S(2)}, u32[]{:S(2)}) collective-permute-start(bf16[8,1024]{1,0:T(8,128)(2,1)S(1)} %collective-permute-done.5), channel_id=1, source_target_pairs={{0,7},{1,0},{2,1},{3,2},{4,3},{5,4},{6,5},{7,6},{8,15},{9,8},{10,9... | collective-permute-start | bytes 49160 | tf_op jit(solution)/shard_map/ppermute | solution.py:21
  37.7 0.8 collective-permute-done.3
  38.6 0.6 collective-permute-done.6
  39.2 20.0 %all-to-all-done = bf16[4,48,4096]{2,1,0:T(8,128)(2,1)S(1)} async-done(((bf16[4,48,4096]{2,1,0:T(8,128)(2,1)}), bf16[4,48,4096]{2,1,0:T(8,128)(2,1)S(1)}, u32[]{:S(2)}, u32[]{:S(2)}) %all-to-all-start) | async-done | bytes 1572896 | tf_op jit(solution)/shard_map/all_to_all | solution.py:46
  59.2 4.8 %fusion.4 = f32[4,3,16,256]{3,2,0,1:T(8,128)S(1)} fusion(bf16[3,256,4096]{2,1,0:T(8,128)(2,1)} %param.10, bf16[4,3,16,4096]{3,2,1,0:T(8,128)(2,1)S(1)} %bitcast.25), kind=kOutput, calls=%fused_computation.8 | convolution fusion | flops 402653184 | bytes 8060928 | tf_op jit(solution)/shard_map/gsmc,sjc->gsmj/dot_general | solution.py:48
  64.0 0.7 copy.23
  64.7 0.0 copy-start.1
  64.7 1.5 %reshape.132 = f32[256,192]{1,0:T(8,128)} reshape(f32[256,3,4,16]{3,2,1,0:T(4,128)S(1)} %bitcast.24) | data formatting | bytes 393216
  66.2 0.0 reduce-scatter.4.cloned.1.call-update
  66.3 15.9 %all_gather.3 = bf16[256,1024]{1,0:T(8,128)(2,1)S(1)} all-gather(bf16[64,1024]{1,0:T(8,128)(2,1)S(1)} %constant_dynamic-slice_fusion), channel_id=1, replica_groups=mesh['grp'=4,'mem'=8] {'grp'}, dimensions={0}, use_global_device_ids=true | all-gather | bytes 655360 | tf_op jit(solution)/shard_map/all_gather | solution.py:25
  82.2 17.0 %reduce-scatter.4.cloned.1.call-done = f32[32,192]{1,0:T(8,128)} async-done(((f32[256,192]{1,0:T(8,128)}), f32[32,192]{1,0:T(8,128)}) %reduce-scatter.4.cloned.1.call-update) | async-done | bytes 24592
  99.2 0.9 reshape.133
  100.1 0.1 copy.20
  100.2 0.7 reshape.140
  100.9 4.6 %all-to-all-start.1 = ((f32[4,1,1536]{2,1,0:T(1,128)}), f32[4,1,1536]{2,1,0:T(1,128)S(1)}, u32[]{:S(2)}, u32[]{:S(2)}) async-start(f32[4,1,1536]{2,1,0:T(1,128)} %reshape.140), calls=%async_computation.1 | async-start | bytes 49152 | tf_op jit(solution)/shard_map/all_to_all | solution.py:52
  105.5 0.0 copy-done.1
  105.5 1.0 fusion.3
  106.5 4.6 %all-to-all-done.1 = f32[4,1,1536]{2,1,0:T(1,128)S(1)} async-done(((f32[4,1,1536]{2,1,0:T(1,128)}), f32[4,1,1536]{2,1,0:T(1,128)S(1)}, u32[]{:S(2)}, u32[]{:S(2)}) %all-to-all-start.1) | async-done | bytes 24608 | tf_op jit(solution)/shard_map/all_to_all | solution.py:52
  111.2 0.5 broadcast.126
  111.7 0.7 reduce
  112.4 0.1 reshape.141
  112.5 0.6 gather_fusion
  113.2 0.1 copy.21
  113.2 0.7 compare_select_fusion
  (23 shorter events, 0.1 us)
Async XLA Ops:
  7.2 2.2 %copy-start = (bf16[64,4096]{1,0:T(8,128)(2,1)S(1)}, bf16[64,4096]{1,0:T(8,128)(2,1)}, u32[]{:S(2)}) copy-start(bf16[64,4096]{1,0:T(8,128)(2,1)} %param.9) | copy-start | bytes 1572868
  15.7 6.5 %copy-start.2 = (bf16[8,1024]{1,0:T(8,128)(2,1)S(1)}, bf16[8,1024]{1,0:T(8,128)(2,1)}, u32[]{:S(2)}) copy-start(bf16[8,1024]{1,0:T(8,128)(2,1)} %param.7) | copy-start | bytes 49156
  15.7 43.4 %all-to-all-start = ((bf16[4,48,4096]{2,1,0:T(8,128)(2,1)}), bf16[4,48,4096]{2,1,0:T(8,128)(2,1)S(1)}, u32[]{:S(2)}, u32[]{:S(2)}) async-start(bf16[4,48,4096]{2,1,0:T(8,128)(2,1)} %bitcast.3), calls=%async_computation | async-start | bytes 3145728 | tf_op jit(solution)/shard_map/all_to_all | solution.py:46
  22.2 77.0 %reduce-scatter.4.cloned.1.call-start = ((), (), s32[]{:S(2)}) async-start(), calls=%async_computation.3 | async-start | bytes 294912
  22.2 4.1 %collective-permute-start = (bf16[8,1024]{1,0:T(8,128)(2,1)S(1)}, bf16[8,1024]{1,0:T(8,128)(2,1)S(1)}, u32[]{:S(2)}, u32[]{:S(2)}) collective-permute-start(bf16[8,1024]{1,0:T(8,128)(2,1)S(1)} %copy-done.2), channel_id=1, source_target_pairs={{0,1},{1,2},{2,3},{3,4},{4,5},{5,6},{6,7},{7,0},{8,9},{9,10},{10,1... | collective-permute-start | bytes 49160 | tf_op jit(solution)/shard_map/ppermute | solution.py:19
  26.3 4.1 %collective-permute-start.1 = (bf16[8,1024]{1,0:T(8,128)(2,1)S(1)}, bf16[8,1024]{1,0:T(8,128)(2,1)S(1)}, u32[]{:S(2)}, u32[]{:S(2)}) collective-permute-start(bf16[8,1024]{1,0:T(8,128)(2,1)S(1)} %collective-permute-done), channel_id=1, source_target_pairs={{0,1},{1,2},{2,3},{3,4},{4,5},{5,6},{6,7},{7,0},{8,9},{9,10},{10,1... | collective-permute-start | bytes 49160 | tf_op jit(solution)/shard_map/ppermute | solution.py:19
  26.3 4.1 %collective-permute-start.4 = (bf16[8,1024]{1,0:T(8,128)(2,1)S(1)}, bf16[8,1024]{1,0:T(8,128)(2,1)S(1)}, u32[]{:S(2)}, u32[]{:S(2)}) collective-permute-start(bf16[8,1024]{1,0:T(8,128)(2,1)S(1)} %copy-done.2), channel_id=1, source_target_pairs={{0,7},{1,0},{2,1},{3,2},{4,3},{5,4},{6,5},{7,6},{8,15},{9,8},{10,9... | collective-permute-start | bytes 49160 | tf_op jit(solution)/shard_map/ppermute | solution.py:21
  30.4 4.1 %collective-permute-start.2 = (bf16[8,1024]{1,0:T(8,128)(2,1)S(1)}, bf16[8,1024]{1,0:T(8,128)(2,1)S(1)}, u32[]{:S(2)}, u32[]{:S(2)}) collective-permute-start(bf16[8,1024]{1,0:T(8,128)(2,1)S(1)} %collective-permute-done.1), channel_id=1, source_target_pairs={{0,1},{1,2},{2,3},{3,4},{4,5},{5,6},{6,7},{7,0},{8,9},{9,10},{10,1... | collective-permute-start | bytes 49160 | tf_op jit(solution)/shard_map/ppermute | solution.py:19
  30.4 4.4 %collective-permute-start.5 = (bf16[8,1024]{1,0:T(8,128)(2,1)S(1)}, bf16[8,1024]{1,0:T(8,128)(2,1)S(1)}, u32[]{:S(2)}, u32[]{:S(2)}) collective-permute-start(bf16[8,1024]{1,0:T(8,128)(2,1)S(1)} %collective-permute-done.4), channel_id=1, source_target_pairs={{0,7},{1,0},{2,1},{3,2},{4,3},{5,4},{6,5},{7,6},{8,15},{9,8},{10,9... | collective-permute-start | bytes 49160 | tf_op jit(solution)/shard_map/ppermute | solution.py:21
  34.5 4.1 %collective-permute-start.3 = (bf16[8,1024]{1,0:T(8,128)(2,1)S(1)}, bf16[8,1024]{1,0:T(8,128)(2,1)S(1)}, u32[]{:S(2)}, u32[]{:S(2)}) collective-permute-start(bf16[8,1024]{1,0:T(8,128)(2,1)S(1)} %collective-permute-done.2), channel_id=1, source_target_pairs={{0,1},{1,2},{2,3},{3,4},{4,5},{5,6},{6,7},{7,0},{8,9},{9,10},{10,1... | collective-permute-start | bytes 49160 | tf_op jit(solution)/shard_map/ppermute | solution.py:19
  34.8 4.4 %collective-permute-start.6 = (bf16[8,1024]{1,0:T(8,128)(2,1)S(1)}, bf16[8,1024]{1,0:T(8,128)(2,1)S(1)}, u32[]{:S(2)}, u32[]{:S(2)}) collective-permute-start(bf16[8,1024]{1,0:T(8,128)(2,1)S(1)} %collective-permute-done.5), channel_id=1, source_target_pairs={{0,7},{1,0},{2,1},{3,2},{4,3},{5,4},{6,5},{7,6},{8,15},{9,8},{10,9... | collective-permute-start | bytes 49160 | tf_op jit(solution)/shard_map/ppermute | solution.py:21
  64.7 40.8 %copy-start.1 = (bf16[256,1024]{1,0:T(8,128)(2,1)S(1)}, bf16[256,1024]{1,0:T(8,128)(2,1)}, u32[]{:S(2)}) copy-start(bf16[256,1024]{1,0:T(8,128)(2,1)} %param.8) | copy-start | bytes 1572868
  100.9 10.2 %all-to-all-start.1 = ((f32[4,1,1536]{2,1,0:T(1,128)}), f32[4,1,1536]{2,1,0:T(1,128)S(1)}, u32[]{:S(2)}, u32[]{:S(2)}) async-start(f32[4,1,1536]{2,1,0:T(1,128)} %reshape.140), calls=%async_computation.1 | async-start | bytes 49152 | tf_op jit(solution)/shard_map/all_to_all | solution.py:52
Sparse Core Ops, SparseCore 0:
  66.3 32.7 reduce-scatter.3
